TPU v7x, 32 devices: a whole 2x2x4 slice. The times are simulated.
32 devices in a mesh: tmpl: 2 (over y), freq: 16 (over z, x, core).
Axes of the slice: x: 2, y: 2, z: 4, core: 2. Of those that a mesh axis runs over, the one named last changes fastest.
Arguments:
- strain: bfloat16 [3, 1024, 512], P(None, 'freq'), may hold values from -6 to 6
- gate_start: int32 [3, 2], replicated, may hold values from 0 to 520191
- psd_inverse: float32 [3, 512, 1024], P(None, 'freq'), may hold values from 0.5 to 6, as said below
- templates: bfloat16 [8, 2, 512, 1024], P('tmpl', None, 'freq'), may hold values from -6 to 6
- basis: bfloat16 [3, 4, 512, 1024], P(None, None, 'freq'), may hold values from -2.5 to 4.5
Outputs:
- best: float32 [512, 1024], P('tmpl', 'freq')
Inputs may be any that keep to these rules, and one draw needn't show every extreme that they name: `psd_inverse`: positive weights.
All inputs are finite; a program needn't handle non-finite values.
Results may differ from a plain program's by a relative error of at most 0.004.
Values may be sent and summed in bfloat16 or wider, within the bound.
No kernel may reach another device: no remote copies, remote signals or barrier semaphores. Data moves between devices by JAX's collectives and lax.ppermute only.
A program may use at most 128 MiB of HBM per device.

v0:
```python
import math
import jax
import jax.numpy as jnp
from jax import lax
from jax.sharding import PartitionSpec as P

N1 = 512
N2 = 1024
DET = 3
RESP = 5
GATE_LEN = 4096


def fourier_table(length, orient):
    indices = jnp.arange(length, dtype=jnp.int32)
    products = indices[:, None] * indices[None, :] % length
    angles = products.astype(jnp.float32) * (2.0 * math.pi / length)
    return (jnp.cos(angles), orient * jnp.sin(angles))


def real_table(length):
    cosines, sine_part = fourier_table(length, -1.0)
    return jnp.concatenate([cosines, sine_part], axis=1).astype(jnp.bfloat16)


def complex_table(length, orient):
    cosines, sine_part = fourier_table(length, orient)
    upper_row = jnp.concatenate([cosines, sine_part], axis=1)
    bottom = jnp.concatenate([-sine_part, cosines], axis=1)
    return jnp.stack([upper_row, bottom], axis=0).astype(jnp.bfloat16)


def twiddle_table(row_index, col_index, modulus, orient):
    products = row_index[:, None] * col_index[None, :] % modulus
    angles = products.astype(jnp.float32) * (2.0 * math.pi / modulus)
    return (jnp.cos(angles), orient * jnp.sin(angles))


def rotate(real_part, imag_part, cosines, sine_part):
    return (
        real_part * cosines - imag_part * sine_part,
        real_part * sine_part + imag_part * cosines,
    )


def statistic(real_lags, imag_lags, variance, projection, spread):
    base_real = real_lags[:, 0]
    base_imag = imag_lags[:, 0]
    head_term = (base_real * base_real + base_imag * base_imag) / (
        N1 * N2 * variance[:, None, None]
    )
    remain_real = real_lags[:, 1:] - projection[:, :, None, None] * base_real[:, None]
    remain_imag = imag_lags[:, 1:] - projection[:, :, None, None] * base_imag[:, None]
    tail_term = jnp.sum(
        (remain_real * remain_real + remain_imag * remain_imag) / spread[:, :, None, None], axis=1
    )
    return jnp.sum(head_term + tail_term, axis=0) / (DET * RESP)


def on_device(strain, gate_start, psd_inverse, templates, basis):
    freq_place = lax.axis_index("freq")
    local_cols = strain.shape[1]
    local_rows = psd_inverse.shape[1]
    modulus = N1 * N2
    col_global = freq_place * local_cols + jnp.arange(local_cols, dtype=jnp.int32)
    sample = N2 * jnp.arange(N1, dtype=jnp.int32)[None, :] + col_global[:, None]
    starts = gate_start[:, :, None, None]
    inside = (sample[None, None] >= starts) & (sample[None, None] < starts + GATE_LEN)
    keep_mask = jnp.where(jnp.any(inside, axis=1), 0.0, 1.0).astype(strain.dtype)
    gated_strain = strain * keep_mask
    section = jnp.einsum(
        "dcn,nq->dqc", gated_strain, real_table(N1), preferred_element_type=jnp.float32
    )
    section = section.reshape(DET, 2, N1, local_cols)
    cosines, sine_part = twiddle_table(jnp.arange(N1, dtype=jnp.int32), col_global, modulus, -1.0)
    real_part, imag_part = rotate(section[:, 0], section[:, 1], cosines, sine_part)
    section_one = jnp.stack([real_part, imag_part], axis=1).astype(jnp.bfloat16)
    spectra = lax.all_to_all(section_one, "freq", split_axis=2, concat_axis=3, tiled=True)
    spectrum = jnp.einsum(
        "dpkc,pcq->dkq", spectra, complex_table(N2, -1.0), preferred_element_type=jnp.float32
    )
    data_real = spectrum[..., :N2] * psd_inverse
    data_imag = spectrum[..., N2:] * psd_inverse
    basis_float = basis.astype(jnp.float32)
    responses = jnp.concatenate(
        [jnp.ones((DET, 1, local_rows, N2), jnp.float32), basis_float], axis=1
    )
    template_real = templates[:, 0].astype(jnp.float32)
    template_imag = templates[:, 1].astype(jnp.float32)
    template_count = templates.shape[0]
    product_real = (
        data_real[None] * template_real[:, None] + data_imag[None] * template_imag[:, None]
    )
    product_imag = (
        data_imag[None] * template_real[:, None] - data_real[None] * template_imag[:, None]
    )
    filtered = jnp.stack(
        [product_real[:, :, None] * responses[None], product_imag[:, :, None] * responses[None]],
        axis=3,
    )
    filtered = filtered.astype(jnp.bfloat16).reshape(-1, 2, local_rows, N2)
    lag_section = jnp.einsum(
        "ipkm,pmq->ikq", filtered, complex_table(N2, 1.0), preferred_element_type=jnp.float32
    )
    row_global = freq_place * local_rows + jnp.arange(local_rows, dtype=jnp.int32)
    back_cos, back_sin = twiddle_table(row_global, jnp.arange(N2, dtype=jnp.int32), modulus, 1.0)
    real_part, imag_part = rotate(lag_section[..., :N2], lag_section[..., N2:], back_cos, back_sin)
    lag_one = jnp.stack([real_part, imag_part], axis=1).astype(jnp.bfloat16)
    table_row = complex_table(N1, 1.0)
    lags = jnp.einsum(
        "ipkc,pkq->iqc",
        lax.all_to_all(lag_one, "freq", split_axis=3, concat_axis=2, tiled=True),
        table_row,
        preferred_element_type=jnp.float32,
    )
    weight = (psd_inverse * psd_inverse)[None] * (
        template_real * template_real + template_imag * template_imag
    )[:, None]
    variance_local = jnp.sum(weight, axis=(2, 3))
    intersection_local = jnp.einsum("tdkm,djkm->tdj", weight, basis_float)
    variance, intersection = lax.psum((variance_local, intersection_local), "freq")
    projection = intersection / variance[..., None]
    centred = basis_float[None] - projection[..., None, None]
    spread_local = jnp.sum(weight[:, :, None] * centred * centred, axis=(3, 4))
    spread = modulus * lax.psum(spread_local, "freq")
    batched = jax.vmap(statistic)
    lag_grid = lags.reshape(template_count, DET, RESP, 2, N1, local_cols)
    statistics = batched(lag_grid[:, :, :, 0], lag_grid[:, :, :, 1], variance, projection, spread)
    best_local = jnp.max(statistics, axis=0)
    received = lax.all_to_all(best_local[None], "tmpl", split_axis=1, concat_axis=0, tiled=True)
    return jnp.max(received, axis=0)


def solution(mesh):
    placed = (
        P(None, "freq", None),
        P(),
        P(None, "freq", None),
        P("tmpl", None, "freq", None),
        P(None, None, "freq", None),
    )
    return jax.shard_map(
        on_device, mesh=mesh, in_specs=placed, out_specs=P("tmpl", "freq"), check_vma=False
    )
```

profile of v0, /device:TPU:0, one launch (start us, length us, event | category | flops | bytes accessed | tf_op | source)
XLA Modules:
  0.0 587.6 jit_solution(1520136712507840119)
XLA Ops:
  0.0 4.3 multiply_convert_fusion.3
  16.8 8.0 %all-to-all-start = ((bf16[16,2,6144]{2,1,0:T(2,128)(2,1)}), bf16[16,2,6144]{2,1,0:T(2,128)(2,1)}, u32[]{:S(2)}, u32[]{:S(2)}) async-start(bf16[16,2,6144]{2,1,0:T(2,128)(2,1)} %reshape.229), calls=%async_computation | async-start | bytes 786432 | tf_op jit(solution)/shard_map/all_to_all | solution.py:78
  24.8 16.6 %negate_convert_fusion = (bf16[1024,1024]{1,0:T(8,128)(2,1)S(1)}, bf16[1024,1024]{1,0:T(8,128)(2,1)}) fusion(), kind=kLoop, calls=%fused_computation.41 | loop fusion | flops 19922944 | bytes 4194304 | tf_op jit(solution)/shard_map/convert.7
  41.5 17.8 %cosine_convert_fusion = (bf16[1024,1024]{1,0:T(8,128)(2,1)}, bf16[1024,1024]{1,0:T(8,128)(2,1)}) fusion(), kind=kLoop, calls=%fused_computation.43 | loop fusion | flops 17825792 | bytes 4194304 | tf_op jit(solution)/shard_map/convert.22
  59.3 16.4 %fusion.32 = bf16[1024,1024]{1,0:T(8,128)(2,1)} fusion(), kind=kLoop, calls=%fused_computation.55 | loop fusion | flops 15728640 | bytes 2097152 | tf_op jit(solution)/shard_map/convert.11
  79.4 9.4 %fusion.18 = (bf16[1,1024,2048]{2,1,0:T(8,128)(2,1)}, bf16[1,1024,2048]{2,1,0:T(8,128)(2,1)}, bf16[1,1024,2048]{2,1,0:T(8,128)(2,1)}, bf16[1,1024,2048]{2,1,0:T(8,128)(2,1)}) fusion(bf16[1024,1024]{1,0:T(8,128)(2,1)} %get-tuple-element.38, bf16[1024,1024]{1,0:T(8,128)(2,1)} %get-tuple-element.39, bf16[1024,1024]{1,0:T(8,128)(2,1)S(1)} %get-tuple-element.36, ...), kind=kLoop, calls=%fused_computation.36 | loop fusion | flops 29360128 | bytes 27262976 | tf_op jit(solution)/shard_map/stack | solution.py:30
  92.4 4.4 fusion.28
  98.5 5.6 multiply_convert_fusion.1
  104.1 18.9 %fusion.13 = f32[60,32,2048]{2,1,0:T(8,128)S(1)} fusion(bf16[1,1024,2048]{2,1,0:T(8,128)(2,1)S(1)} %copy-done.2, bf16[1,1024,2048]{2,1,0:T(8,128)(2,1)S(1)} %copy-done.3, bf16[60,1,32,1024]{3,2,1,0:T(8,128)(2,1)} %bitcast.107, bf16[60,1,32,1024]{3,2,1,0:T(8,128)(2,1)} %bitcast.106), kind=kOutput, calls=%fused_computation.29 | convolution fusion | flops 16114253824 | bytes 31981568 | tf_op jit(solution)/shard_map/ipkm,pmq->ikq/dot_general | solution.py:102
  125.7 3.7 pad_maximum_fusion
  129.4 28.5 %copy.95 = bf16[60,2,32,1024]{0,2,1,3:T(8,128)(2,1)} copy(bf16[60,2,32,1024]{3,2,0,1:T(8,128)(2,1)} %pad_maximum_fusion) | data formatting | bytes 15728640 | tf_op jit(solution)/shard_map/stack | solution.py:108
  157.9 46.8 %reshape.231 = bf16[16,2,122880]{2,1,0:T(2,128)(2,1)} reshape(bf16[1024,2,32,60]{3,2,1,0:T(8,128)(2,1)} %bitcast.97) | data formatting | bytes 15728640
  204.6 6.3 %all-to-all-start.1 = ((bf16[16,2,122880]{2,1,0:T(2,128)(2,1)}), bf16[16,2,122880]{2,1,0:T(2,128)(2,1)}, u32[]{:S(2)}, u32[]{:S(2)}) async-start(bf16[16,2,122880]{2,1,0:T(2,128)(2,1)} %reshape.231), calls=%async_computation.1 | async-start | bytes 15728640 | tf_op jit(solution)/shard_map/all_to_all | solution.py:112
  211.6 4.0 negate_convert_fusion.2
  219.6 154.7 %all-reduce.1 = (f32[4,3,4]{2,0,1:T(4,128)S(1)}, f32[4,3]{0,1:T(4,128)S(1)}) all-reduce(f32[4,3,4]{2,0,1:T(4,128)S(1)} %fusion.35, f32[4,3]{0,1:T(4,128)S(1)} %get-tuple-element.24), channel_id=1, replica_groups=mesh['tmpl'=2,'freq'=16] {'freq'}, use_global_device_ids=true, to_apply=%region_3.4 | all-reduce | flops 60 | bytes 480 | tf_op jit(solution)/shard_map/psum | solution.py:121
  376.4 51.9 %psum.23 = f32[4,3,4]{2,0,1:T(4,128)S(1)} all-reduce(f32[4,3,4]{2,0,1:T(4,128)S(1)} %copy.106), channel_id=1, replica_groups=mesh['tmpl'=2,'freq'=16] {'freq'}, use_global_device_ids=true, to_apply=%region_5.6 | all-reduce | flops 48 | bytes 384 | tf_op jit(solution)/shard_map/psum | solution.py:125
  428.6 53.3 %reshape.232 = bf16[1024,2,32,60]{3,2,1,0:T(8,128)(2,1)} reshape(bf16[16,2,122880]{2,1,0:T(2,128)(2,1)} %all-to-all-done.1) | data formatting | bytes 15728640
  481.9 31.2 %copy.96 = bf16[60,2,32,16,64]{4,2,3,1,0:T(8,128)(2,1)} copy(bf16[60,2,32,16,64]{0,2,1,4,3:T(8,128)(2,1)} %bitcast.98) | data formatting | bytes 15728640 | tf_op jit(solution)/shard_map/all_to_all | solution.py:112
  513.1 15.0 %convolution_bitcast_fusion = f32[60,1024,64]{1,2,0:T(8,128)} fusion(bf16[60,2,512,64]{3,2,1,0:T(8,128)(2,1)} %bitcast.105, bf16[1,512,1024]{2,1,0:T(8,128)(2,1)S(1)} %copy-done.12, bf16[1,512,1024]{2,1,0:T(8,128)(2,1)S(1)} %copy-done.11), kind=kOutput, calls=%fused_computation.1 | convolution fusion | flops 8057257984 | bytes 25690112 | tf_op jit(solution)/shard_map/ipkc,pkq->iqc/dot_general | solution.py:110
  528.0 20.8 %reshape.220 = f32[4,3,5,2,512,64]{4,3,5,2,1,0:T(2,128)} reshape(f32[60,1024,64]{1,2,0:T(8,128)} %convolution_bitcast_fusion) | data formatting | bytes 31457280 | tf_op jit(solution)/shard_map/reshape | solution.py:127
  548.9 17.2 %fusion.80 = (f32[4,3,5,1,512,64]{4,3,5,2,1,0:T(1,128)S(1)}, f32[4,3,5,1,512,64]{4,3,5,2,1,0:T(1,128)}) fusion(f32[4,3,5,2,512,64]{4,3,5,2,1,0:T(2,128)} %reshape.220), kind=kLoop, calls=%fused_computation.143 | loop fusion | bytes 31457280 | tf_op jit(solution)/shard_map/slice | solution.py:128
  566.1 4.3 copy.123
  572.4 2.7 fusion.12
  578.0 7.1 %all_to_all.48 = f32[2,1,16384]{2,1,0:T(1,128)S(1)} all-to-all(f32[2,1,16384]{2,1,0:T(1,128)S(1)} %reshape.233), channel_id=1, replica_groups=mesh['tmpl'=2,'freq'=16] {'tmpl'}, dimensions={0} | all-to-all | bytes 262144 | tf_op jit(solution)/shard_map/all_to_all | solution.py:130
  (88 shorter events, 37.7 us)
Async XLA Ops:
  4.4 3.0 copy-start.8
  16.8 72.0 %all-to-all-start = ((bf16[16,2,6144]{2,1,0:T(2,128)(2,1)}), bf16[16,2,6144]{2,1,0:T(2,128)(2,1)}, u32[]{:S(2)}, u32[]{:S(2)}) async-start(bf16[16,2,6144]{2,1,0:T(2,128)(2,1)} %reshape.229), calls=%async_computation | async-start | bytes 786432 | tf_op jit(solution)/shard_map/all_to_all | solution.py:78
  24.8 50.8 %copy-start.6 = (bf16[4,2,32,1024]{3,2,1,0:T(8,128)(2,1)S(1)}, bf16[4,2,32,1024]{3,2,1,0:T(8,128)(2,1)}, u32[]{:S(2)}) copy-start(bf16[4,2,32,1024]{3,2,1,0:T(8,128)(2,1)} %param.8) | copy-start | bytes 1572868
  41.5 36.4 %copy-start.4 = (bf16[3,4,32,1024]{3,2,1,0:T(8,128)(2,1)S(1)}, bf16[3,4,32,1024]{3,2,1,0:T(8,128)(2,1)}, u32[]{:S(2)}) copy-start(bf16[3,4,32,1024]{3,2,1,0:T(8,128)(2,1)} %param.9) | copy-start | bytes 2359300
  76.6 2.8 copy-start
  92.4 4.4 copy-start.14
  92.4 5.3 copy-start.5
  96.8 1.7 copy-start.1
  98.5 5.6 copy-start.2
  98.5 5.6 copy-start.3
  104.1 18.9 %copy-start.13 = (f32[32,1024]{1,0:T(8,128)S(1)}, f32[32,1024]{1,0:T(8,128)}, u32[]{:S(2)}) copy-start(f32[32,1024]{1,0:T(8,128)} %get-tuple-element.33) | copy-start | bytes 393220
  204.6 6.5 %copy-start.7 = (bf16[4,2,32,1024]{3,2,1,0:T(8,128)(2,1)S(1)}, bf16[4,2,32,1024]{3,2,1,0:T(8,128)(2,1)}, u32[]{:S(2)}) copy-start(bf16[4,2,32,1024]{3,2,1,0:T(8,128)(2,1)} %param.8) | copy-start | bytes 1572868
  204.6 224.0 %all-to-all-start.1 = ((bf16[16,2,122880]{2,1,0:T(2,128)(2,1)}), bf16[16,2,122880]{2,1,0:T(2,128)(2,1)}, u32[]{:S(2)}, u32[]{:S(2)}) async-start(bf16[16,2,122880]{2,1,0:T(2,128)(2,1)} %reshape.231), calls=%async_computation.1 | async-start | bytes 15728640 | tf_op jit(solution)/shard_map/all_to_all | solution.py:112
  210.9 4.7 copy-start.9
  210.9 6.3 %copy-start.10 = (f32[3,32,1024]{2,1,0:T(8,128)S(1)}, f32[3,32,1024]{2,1,0:T(8,128)}, u32[]{:S(2)}) copy-start(f32[3,32,1024]{2,1,0:T(8,128)} %get-tuple-element.25) | copy-start | bytes 1179652
  481.9 31.2 %copy-start.11 = (bf16[1,512,1024]{2,1,0:T(8,128)(2,1)S(1)}, bf16[1,512,1024]{2,1,0:T(8,128)(2,1)}, u32[]{:S(2)}) copy-start(bf16[1,512,1024]{2,1,0:T(8,128)(2,1)} %get-tuple-element.28) | copy-start | bytes 3145732
  481.9 31.2 %copy-start.12 = (bf16[1,512,1024]{2,1,0:T(8,128)(2,1)S(1)}, bf16[1,512,1024]{2,1,0:T(8,128)(2,1)}, u32[]{:S(2)}) copy-start(bf16[1,512,1024]{2,1,0:T(8,128)(2,1)} %get-tuple-element.29) | copy-start | bytes 3145732
where the time goes:
time: 595 us; the launch traced here: 588 us
  local copies, waits for them, and re-layouts  218 us (37%)
  blocking collectives  214 us (36%)
  other arithmetic  99.8 us (17%)
  matrix products  41 us (7%)
  starting transfers between devices  14.3 us (2%)
    psum x1, blocking collectives, on_device(): lax.psum((variance_local, intersection_local), 'freq')  155 us
    unnamed x42, local copies, waits for them, and re-layouts  114 us
    another operation x7, other arithmetic  66.4 us
    psum x1, blocking collectives, on_device(): spread = modulus * lax.psum(spread_local, 'freq')  51.9 us
    all_to_all x1, local copies, waits for them, and re-layouts, on_device(): lax.all_to_all(lag_one, 'freq', split_axis=3, concat_axis=2, tiled=True)  31.2 us
    another operation x1, local copies, waits for them, and re-layouts, on_device(): lag_one = jnp.stack([real_part, imag_part], axis=1).astype(jnp.bfloat16)  28.5 us
    reshape x1, local copies, waits for them, and re-layouts, on_device(): lag_grid = lags.reshape(template_count, DET, RESP, 2, N1, local_cols)  20.8 us
    dot_general x1, matrix products, on_device(): jnp.einsum('ipkm,pmq->ikq', filtered, complex_table(N2, 1.0), preferred_e...  18.9 us
  transfers between devices with their start and end apart: 2, of which 0 were waited for; matrix products, arithmetic and copies ran while one was open for 13% of the time, Pallas kernels for 0%

commit v1 on v0

--- a/solution.py
+++ b/solution.py
@@ -3,6 +3,7 @@
 import jax.numpy as jnp
 from jax import lax
 from jax.sharding import PartitionSpec as P
+from jax.lax import all_to_all, axis_size
 
 N1 = 512
 N2 = 1024
@@ -107,11 +108,17 @@
     real_part, imag_part = rotate(lag_section[..., :N2], lag_section[..., N2:], back_cos, back_sin)
     lag_one = jnp.stack([real_part, imag_part], axis=1).astype(jnp.bfloat16)
     table_row = complex_table(N1, 1.0)
+    meet_lane_now = lambda z_in, at_axis, join_dim: jnp.concatenate(
+        all_to_all(
+            jnp.stack(jnp.split(z_in, axis_size("freq"), at_axis)),
+            concat_axis=0,
+            axis_name="freq",
+            split_axis=0,
+        ),
+        axis=join_dim,
+    )
     lags = jnp.einsum(
-        "ipkc,pkq->iqc",
-        lax.all_to_all(lag_one, "freq", split_axis=3, concat_axis=2, tiled=True),
-        table_row,
-        preferred_element_type=jnp.float32,
+        "ipkc,pkq->iqc", meet_lane_now(lag_one, 3, 2), table_row, preferred_element_type=jnp.float32
     )
     weight = (psd_inverse * psd_inverse)[None] * (
         template_real * template_real + template_imag * template_imag

time: 595 us -> 499 us (0.84)
  local copies, waits for them, and re-layouts: 218 us -> 118 us
    unnamed x42, local copies, waits for them, and re-layouts: 114 us -> 56.4 us
    all_to_all x1 -> x0, local copies, waits for them, and re-layouts: 31.2 us -> none  [on_device(): lax.all_to_all(lag_one, 'freq', split_axis=3, concat_axis=2, tiled=True)]
    another operation x1 -> x0, local copies, waits for them, and re-layouts: 28.5 us -> none  [on_device(): lag_one = jnp.stack([real_part, imag_part], axis=1).astype(jnp.bfloat16)]
    reshape x0 -> x2, local copies, waits for them, and re-layouts: none -> 16.7 us  [on_device(): jnp.concatenate(all_to_all(jnp.stack(jnp.split(z_in, axis_size('freq'), a...]
    unnamed x2 -> x17, other arithmetic: 3.38 us -> 9.89 us
    another operation x7 -> x8, other arithmetic: 66.4 us -> 67 us
  transfers between devices with their start and end apart: 2 -> 2, of which waited for: 0 -> 0; matrix products, arithmetic and copies ran while one was open for 13% -> 15% of each run, Pallas kernels for 0% -> 0%
where the time goes in v1:
time: 499 us; the launch traced here: 491 us
  blocking collectives  214 us (43%)
  local copies, waits for them, and re-layouts  118 us (24%)
  other arithmetic  103 us (21%)
  matrix products  42.6 us (9%)
  starting transfers between devices  14.1 us (3%)
    psum x1, blocking collectives, on_device(): lax.psum((variance_local, intersection_local), 'freq')  155 us
    another operation x7, other arithmetic  66.4 us
    unnamed x42, local copies, waits for them, and re-layouts  56.4 us
    psum x1, blocking collectives, on_device(): spread = modulus * lax.psum(spread_local, 'freq')  51.9 us
    reshape x1, local copies, waits for them, and re-layouts, on_device(): lag_grid = lags.reshape(template_count, DET, RESP, 2, N1, local_cols)  20.9 us
    dot_general x1, matrix products, on_device(): jnp.einsum('ipkm,pmq->ikq', filtered, complex_table(N2, 1.0), preferred_e...  20.3 us
    slice x1, local copies, waits for them, and re-layouts, on_device(): lag_grid[:, :, :, 0]  17.1 us
    reshape x2, local copies, waits for them, and re-layouts, on_device(): jnp.concatenate(all_to_all(jnp.stack(jnp.split(z_in, axis_size('freq'), a...  16.7 us
  transfers between devices with their start and end apart: 2, of which 0 were waited for; matrix products, arithmetic and copies ran while one was open for 15% of the time, Pallas kernels for 0%

profile of v1, /device:TPU:0, one launch (start us, length us, event | category | flops | bytes accessed | tf_op | source)
XLA Modules:
  0.0 491.5 jit_solution(1415033704592700640)
XLA Ops:
  0.0 4.3 multiply_convert_fusion.3
  16.8 7.6 %all-to-all-start = ((bf16[16,2,6144]{2,1,0:T(2,128)(2,1)}), bf16[16,2,6144]{2,1,0:T(2,128)(2,1)}, u32[]{:S(2)}, u32[]{:S(2)}) async-start(bf16[16,2,6144]{2,1,0:T(2,128)(2,1)} %reshape.237), calls=%async_computation | async-start | bytes 786432 | tf_op jit(solution)/shard_map/all_to_all | solution.py:79
  24.5 16.6 %negate_convert_fusion = (bf16[1024,1024]{1,0:T(8,128)(2,1)S(1)}, bf16[1024,1024]{1,0:T(8,128)(2,1)}) fusion(), kind=kLoop, calls=%fused_computation.70 | loop fusion | flops 19922944 | bytes 4194304 | tf_op jit(solution)/shard_map/convert.7
  41.1 17.8 %cosine_convert_fusion = (bf16[1024,1024]{1,0:T(8,128)(2,1)}, bf16[1024,1024]{1,0:T(8,128)(2,1)}) fusion(), kind=kLoop, calls=%fused_computation.72 | loop fusion | flops 17825792 | bytes 4194304 | tf_op jit(solution)/shard_map/convert.22
  58.9 16.4 %fusion.32 = bf16[1024,1024]{1,0:T(8,128)(2,1)} fusion(), kind=kLoop, calls=%fused_computation.84 | loop fusion | flops 15728640 | bytes 2097152 | tf_op jit(solution)/shard_map/convert.11
  78.6 9.4 %fusion.18 = (bf16[1,1024,2048]{2,1,0:T(8,128)(2,1)}, bf16[1,1024,2048]{2,1,0:T(8,128)(2,1)}, bf16[1,1024,2048]{2,1,0:T(8,128)(2,1)}, bf16[1,1024,2048]{2,1,0:T(8,128)(2,1)}) fusion(bf16[1024,1024]{1,0:T(8,128)(2,1)} %get-tuple-element.38, bf16[1024,1024]{1,0:T(8,128)(2,1)} %get-tuple-element.39, bf16[1024,1024]{1,0:T(8,128)(2,1)S(1)} %get-tuple-element.36, ...), kind=kLoop, calls=%fused_computation.65 | loop fusion | flops 29360128 | bytes 27262976 | tf_op jit(solution)/shard_map/stack | solution.py:31
  91.6 4.4 fusion.28
  97.7 5.6 %multiply_convert_fusion.1 = (bf16[4,3,5,32,1024]{4,3,2,1,0:T(8,128)(2,1)}, bf16[4,3,5,32,1024]{4,3,2,1,0:T(8,128)(2,1)}) fusion(f32[3,5,32,1024]{3,2,1,0:T(8,128)S(1)} %copy-done.2, f32[4,3,32,1024]{3,2,1,0:T(8,128)S(1)} %get-tuple-element.19, f32[4,3,32,1024]{3,2,1,0:T(8,128)S(1)} %get-tuple-element.20), kind=kLoop, calls=%fused_computation.46 | loop fusion | flops 7864320 | bytes 12976128 | tf_op jit(solution)/shard_map/convert.15
  103.3 20.3 %fusion.13 = f32[60,32,2048]{2,1,0:T(8,128)S(1)} fusion(bf16[1,1024,2048]{2,1,0:T(8,128)(2,1)S(1)} %copy-done.3, bf16[1,1024,2048]{2,1,0:T(8,128)(2,1)} %get-tuple-element.13, bf16[60,1,32,1024]{3,2,1,0:T(8,128)(2,1)} %bitcast.140, bf16[60,1,32,1024]{3,2,1,0:T(8,128)(2,1)} %bitcast.139), kind=kOutput, calls=%fused_computation.58 | convolution fusion | flops 16114253824 | bytes 31981568 | tf_op jit(solution)/shard_map/ipkm,pmq->ikq/dot_general | solution.py:103
  123.6 2.8 fusion.26
  133.6 5.5 %copy-done = bf16[16,60,2,32,64]{4,3,1,2,0:T(8,128)(2,1)} copy-done((bf16[16,60,2,32,64]{4,3,1,2,0:T(8,128)(2,1)}, bf16[16,60,2,32,64]{4,3,1,2,0:T(8,128)(2,1)S(1)}, u32[]{:S(2)}) %copy-start) | copy-done | bytes 7864344
  139.1 18.7 %reshape.239 = bf16[16,2,122880]{2,1,0:T(2,128)(2,1)} reshape(bf16[16,2,60,32,64]{4,3,2,1,0:T(8,128)(2,1)} %bitcast.137) | data formatting | bytes 15728640
  157.9 6.5 %all-to-all-start.1 = ((bf16[16,2,122880]{2,1,0:T(2,128)(2,1)}), bf16[16,2,122880]{2,1,0:T(2,128)(2,1)}, u32[]{:S(2)}, u32[]{:S(2)}) async-start(bf16[16,2,122880]{2,1,0:T(2,128)(2,1)} %reshape.239), calls=%async_computation.1 | async-start | bytes 15728640 | tf_op jit(solution)/shard_map/all_to_all | solution.py:112
  165.0 4.0 negate_convert_fusion.2
  173.0 154.6 %all-reduce.1 = (f32[4,3,4]{2,0,1:T(4,128)S(1)}, f32[4,3]{0,1:T(4,128)S(1)}) all-reduce(f32[4,3,4]{2,0,1:T(4,128)S(1)} %fusion.35, f32[4,3]{0,1:T(4,128)S(1)} %get-tuple-element.24), channel_id=1, replica_groups=mesh['tmpl'=2,'freq'=16] {'freq'}, use_global_device_ids=true, to_apply=%region_3.4 | all-reduce | flops 60 | bytes 480 | tf_op jit(solution)/shard_map/psum | solution.py:128
  329.8 51.9 %psum.23 = f32[4,3,4]{2,0,1:T(4,128)S(1)} all-reduce(f32[4,3,4]{2,0,1:T(4,128)S(1)} %copy.101), channel_id=1, replica_groups=mesh['tmpl'=2,'freq'=16] {'freq'}, use_global_device_ids=true, to_apply=%region_5.6 | all-reduce | flops 48 | bytes 384 | tf_op jit(solution)/shard_map/psum | solution.py:132
  382.0 18.5 %reshape.240 = bf16[16,2,60,32,64]{4,3,2,1,0:T(8,128)(2,1)} reshape(bf16[16,2,122880]{2,1,0:T(2,128)(2,1)} %all-to-all-done.1) | data formatting | bytes 15728640
  400.5 8.7 %bitcast_bitcast_fusion = bf16[60,2,16,32,64]{4,3,0,1,2:T(8,128)(2,1)S(1)} fusion(bf16[16,2,60,32,64]{4,3,2,1,0:T(8,128)(2,1)} %reshape.240), kind=kLoop, calls=%fused_computation.207 | loop fusion | bytes 15728640 | tf_op jit(solution)/shard_map/reshape | solution.py:111
  409.2 8.0 %copy.91 = bf16[60,2,16,32,64]{4,3,2,1,0:T(8,128)(2,1)} copy(bf16[60,2,16,32,64]{4,3,0,1,2:T(8,128)(2,1)S(1)} %bitcast_bitcast_fusion) | data formatting | bytes 15728640 | tf_op jit(solution)/shard_map/reshape | solution.py:111
  417.2 15.1 %convolution_bitcast_fusion = f32[60,1024,64]{1,2,0:T(8,128)} fusion(bf16[60,2,512,64]{3,2,1,0:T(8,128)(2,1)} %bitcast.138, bf16[1,512,1024]{2,1,0:T(8,128)(2,1)S(1)} %copy-done.13, bf16[1,512,1024]{2,1,0:T(8,128)(2,1)S(1)} %copy-done.12), kind=kOutput, calls=%fused_computation.31 | convolution fusion | flops 8057257984 | bytes 25690112 | tf_op jit(solution)/shard_map/ipkc,pkq->iqc/dot_general | solution.py:120
  432.3 20.9 %reshape.228 = f32[4,3,5,2,512,64]{4,3,5,2,1,0:T(2,128)} reshape(f32[60,1024,64]{1,2,0:T(8,128)} %convolution_bitcast_fusion) | data formatting | bytes 31457280 | tf_op jit(solution)/shard_map/reshape | solution.py:134
  453.2 17.1 %fusion.97 = (f32[4,3,5,1,512,64]{4,3,5,2,1,0:T(1,128)S(1)}, f32[4,3,5,1,512,64]{4,3,5,2,1,0:T(1,128)}) fusion(f32[4,3,5,2,512,64]{4,3,5,2,1,0:T(2,128)} %reshape.228), kind=kLoop, calls=%fused_computation.205 | loop fusion | bytes 31457280 | tf_op jit(solution)/shard_map/slice | solution.py:135
  470.3 4.3 copy.118
  482.1 7.1 %all_to_all.35 = f32[2,1,16384]{2,1,0:T(1,128)S(1)} all-to-all(f32[2,1,16384]{2,1,0:T(1,128)S(1)} %reshape.241), channel_id=1, replica_groups=mesh['tmpl'=2,'freq'=16] {'tmpl'}, dimensions={0} | all-to-all | bytes 262144 | tf_op jit(solution)/shard_map/all_to_all | solution.py:137
  (103 shorter events, 44.4 us)
Async XLA Ops:
  4.4 3.0 copy-start.9
  16.8 71.2 %all-to-all-start = ((bf16[16,2,6144]{2,1,0:T(2,128)(2,1)}), bf16[16,2,6144]{2,1,0:T(2,128)(2,1)}, u32[]{:S(2)}, u32[]{:S(2)}) async-start(bf16[16,2,6144]{2,1,0:T(2,128)(2,1)} %reshape.237), calls=%async_computation | async-start | bytes 786432 | tf_op jit(solution)/shard_map/all_to_all | solution.py:79
  24.5 50.8 %copy-start.7 = (bf16[4,2,32,1024]{3,2,1,0:T(8,128)(2,1)S(1)}, bf16[4,2,32,1024]{3,2,1,0:T(8,128)(2,1)}, u32[]{:S(2)}) copy-start(bf16[4,2,32,1024]{3,2,1,0:T(8,128)(2,1)} %param.8) | copy-start | bytes 1572868
  41.1 36.0 %copy-start.4 = (bf16[3,4,32,1024]{3,2,1,0:T(8,128)(2,1)S(1)}, bf16[3,4,32,1024]{3,2,1,0:T(8,128)(2,1)}, u32[]{:S(2)}) copy-start(bf16[3,4,32,1024]{3,2,1,0:T(8,128)(2,1)} %param.9) | copy-start | bytes 2359300
  76.5 2.2 copy-start.1
  91.6 4.4 copy-start.14
  91.6 5.3 %copy-start.5 = (f32[4,32,1024]{2,1,0:T(8,128)S(1)}, f32[4,32,1024]{2,1,0:T(8,128)}, u32[]{:S(2)}) copy-start(f32[4,32,1024]{2,1,0:T(8,128)} %get-tuple-element.30) | copy-start | bytes 1572868
  91.6 5.3 %copy-start.6 = (f32[4,32,1024]{2,1,0:T(8,128)S(1)}, f32[4,32,1024]{2,1,0:T(8,128)}, u32[]{:S(2)}) copy-start(f32[4,32,1024]{2,1,0:T(8,128)} %get-tuple-element.31) | copy-start | bytes 1572868
  96.0 1.7 copy-start.2
  97.7 5.6 %copy-start.3 = (bf16[1,1024,2048]{2,1,0:T(8,128)(2,1)S(1)}, bf16[1,1024,2048]{2,1,0:T(8,128)(2,1)}, u32[]{:S(2)}) copy-start(bf16[1,1024,2048]{2,1,0:T(8,128)(2,1)} %get-tuple-element.12) | copy-start | bytes 12582916
  133.6 5.5 %copy-start = (bf16[16,60,2,32,64]{4,3,1,2,0:T(8,128)(2,1)}, bf16[16,60,2,32,64]{4,3,1,2,0:T(8,128)(2,1)S(1)}, u32[]{:S(2)}) copy-start(bf16[16,60,2,32,64]{4,3,1,2,0:T(8,128)(2,1)S(1)} %fusion.64) | copy-start | bytes 23592964
  157.9 6.7 %copy-start.8 = (bf16[4,2,32,1024]{3,2,1,0:T(8,128)(2,1)S(1)}, bf16[4,2,32,1024]{3,2,1,0:T(8,128)(2,1)}, u32[]{:S(2)}) copy-start(bf16[4,2,32,1024]{3,2,1,0:T(8,128)(2,1)} %param.8) | copy-start | bytes 1572868
  157.9 224.1 %all-to-all-start.1 = ((bf16[16,2,122880]{2,1,0:T(2,128)(2,1)}), bf16[16,2,122880]{2,1,0:T(2,128)(2,1)}, u32[]{:S(2)}, u32[]{:S(2)}) async-start(bf16[16,2,122880]{2,1,0:T(2,128)(2,1)} %reshape.239), calls=%async_computation.1 | async-start | bytes 15728640 | tf_op jit(solution)/shard_map/all_to_all | solution.py:112
  164.3 4.7 copy-start.10
  164.3 6.3 %copy-start.11 = (f32[3,32,1024]{2,1,0:T(8,128)S(1)}, f32[3,32,1024]{2,1,0:T(8,128)}, u32[]{:S(2)}) copy-start(f32[3,32,1024]{2,1,0:T(8,128)} %get-tuple-element.25) | copy-start | bytes 1179652
  409.2 8.0 %copy-start.12 = (bf16[1,512,1024]{2,1,0:T(8,128)(2,1)S(1)}, bf16[1,512,1024]{2,1,0:T(8,128)(2,1)}, u32[]{:S(2)}) copy-start(bf16[1,512,1024]{2,1,0:T(8,128)(2,1)} %get-tuple-element.28) | copy-start | bytes 3145732
  409.2 8.0 %copy-start.13 = (bf16[1,512,1024]{2,1,0:T(8,128)(2,1)S(1)}, bf16[1,512,1024]{2,1,0:T(8,128)(2,1)}, u32[]{:S(2)}) copy-start(bf16[1,512,1024]{2,1,0:T(8,128)(2,1)} %get-tuple-element.29) | copy-start | bytes 3145732
